TPU v7x, 32 devices: a whole 2x2x4 slice. The times are simulated.
32 devices in a mesh: row: 4 (over y, x), col: 8 (over z, core).
Axes of the slice: x: 2, y: 2, z: 4, core: 2. Of those that a mesh axis runs over, the one named last changes fastest.
Arguments:
- coupling: float32 [4, 4608, 18432], P(None, 'col', 'row'), may hold values from -0.046875 to 0.046875
- energies: float32 [18432], P(('row', 'col')), may hold values from 0.7 to 14.2
- block: float32 [18432, 16], P(('row', 'col')), may hold values from -6 to 6
Outputs:
- basis: float32 [18432, 16], P(('row', 'col'))
- projections: float32 [2, 16, 16], replicated
- factors: float32 [2, 16, 16], replicated
All inputs are finite; a program needn't handle non-finite values.
Results may differ from a plain program's by a relative error of at most 0.0003.
Values sent between devices are 32-bit elements; how exact they have to be, the bound alone decides.
No kernel may reach another device: no remote copies, remote signals or barrier semaphores. Data moves between devices by JAX's collectives and lax.ppermute only.
A program may use at most 128 MiB of HBM per device.

v0:
```python
import jax
import jax.numpy as jnp
from jax import lax
from jax.sharding import PartitionSpec as P

N = 18432
ITERS = 2
precise = lax.Precision.HIGHEST


def combined(moments_local):
    return lax.psum(moments_local, "row")


def on_device(coupling, energies, block):
    segment = block.shape[0]
    width = block.shape[1]
    column = lax.axis_index("col")
    current, energy_rows = (
        lax.all_gather(block, "col", axis=0, tiled=True),
        lax.all_gather(energies, "col", axis=0, tiled=True),
    )
    prior = jnp.zeros_like(current)
    projection_list = []
    factor_list = []
    for section in range(ITERS):
        own_rows = lax.dynamic_slice_in_dim(current, column * segment, segment, 0)
        column_block = current
        spread = lax.all_gather(own_rows, "row", axis=0, tiled=True)
        spread = spread.reshape(coupling.shape[0], segment, width)
        direct = lax.psum_scatter(
            jnp.einsum("aig,gk->aik", coupling, column_block, precision=precise),
            "row",
            scatter_dimension=0,
            tiled=True,
        ).reshape(segment, width)
        partial_value = jnp.einsum("aig,aik->gk", coupling, spread, precision=precise)
        transposed = lax.psum(partial_value, "col")
        direct_rows = lax.all_gather(direct, "col", axis=0, tiled=True)
        product = energy_rows[:, None] * current + direct_rows + transposed
        stacked = jnp.concatenate([current, prior, product], axis=1)
        moments = combined(jnp.einsum("nk,nl->kl", stacked, stacked, precision=precise)) / N
        projection = moments[:width, 2 * width :]
        cross = moments[width : 2 * width, 2 * width :]
        weights = jnp.concatenate([-projection, -cross, jnp.eye(width, dtype=jnp.float32)], axis=0)
        gram_matrix = jnp.dot(
            weights.T, jnp.dot(moments, weights, precision=precise), precision=precise
        )
        factor = jnp.linalg.cholesky(gram_matrix)
        residual = (
            product
            - jnp.dot(current, projection, precision=precise)
            - jnp.dot(prior, cross, precision=precise)
        )
        prior = current
        current = jax.scipy.linalg.solve_triangular(factor, residual.T, lower=True).T
        projection_list.append(projection)
        factor_list.append(factor)
    basis = lax.dynamic_slice_in_dim(current, column * segment, segment, 0)
    return (basis, jnp.stack(projection_list), jnp.stack(factor_list))


def solution(mesh):
    placed = (P(None, "col", "row"), P(("row", "col")), P(("row", "col"), None))
    return jax.shard_map(
        on_device,
        mesh=mesh,
        in_specs=placed,
        out_specs=(P(("row", "col"), None), P(), P()),
        check_vma=False,
    )
```

profile of v0, /device:TPU:0, one launch (start us, length us, event | category | flops | bytes accessed | tf_op | source)
XLA Modules:
  0.0 340.6 jit_solution(8555709565530399333)
XLA Ops:
  8.0 16.3 %all-gather.2 = f32[8,576,16]{1,2,0:T(8,128)S(1)} all-gather(f32[1,576,16]{1,2,0:T(8,128)} %bitcast.93), channel_id=1, replica_groups=mesh['row'=4,'col'=8] {'col'}, dimensions={0}, use_global_device_ids=true | all-gather | bytes 331776 | tf_op jit(solution)/shard_map/all_gather | solution.py:20
  24.6 40.0 %fusion.44 = f32[4,576,16]{1,2,0:T(8,128)} fusion(f32[4,576,4608]{2,1,0:T(8,128)} %param.6, f32[4608,16,1]{0,1,2:T(8,128)S(1)} %reshape.46), kind=kOutput, calls=%fused_computation.77 | convolution fusion | flops 2038431744 | bytes 42909696 | tf_op jit(solution)/shard_map/aig,gk->aik/dot_general | solution.py:32
  64.9 8.8 %all-gather.3 = f32[4,576,16]{1,2,0:T(8,128)S(1)} all-gather(f32[1,576,16]{1,2,0:T(8,128)S(1)} %dynamic-slice_bitcast_fusion.2), channel_id=1, replica_groups=mesh['row'=4,'col'=8] {'row'}, dimensions={0}, use_global_device_ids=true | all-gather | bytes 184320 | tf_op jit(solution)/shard_map/all_gather | solution.py:29
  73.6 24.6 %convolution_bitcast_fusion.3 = f32[4608,16]{0,1:T(8,128)} fusion(f32[4,576,16]{1,2,0:T(8,128)S(1)} %all-gather.3, f32[4,576,4608]{2,1,0:T(8,128)} %param.6), kind=kOutput, calls=%fused_computation.9 | convolution fusion | flops 2038431744 | bytes 42909696 | tf_op jit(solution)/shard_map/aig,aik->gk/dot_general | solution.py:37
  99.9 27.3 %all-reduce = f32[4608]{0:T(1024)S(1)} all-reduce(f32[4608]{0:T(1024)S(1)} %dynamic-update-slice.2), channel_id=1, replica_groups=mesh['row'=4,'col'=8] {'col'}, use_global_device_ids=true, to_apply=%add | all-reduce | flops 4608 | bytes 36864
  127.2 0.9 copy.10
  128.2 24.6 %all-gather = f32[1,4608,16]{2,0,1:T(1,128)S(1)} all-gather(f32[1,576,16]{2,0,1:T(1,128)S(1)} %copy.10), channel_id=2, replica_groups=mesh['row'=4,'col'=8] {'col'}, dimensions={1}, use_global_device_ids=true | all-gather | bytes 331776 | tf_op jit(solution)/shard_map/all_gather | solution.py:39
  152.7 2.2 copy.11
  154.9 1.0 fusion.19
  156.0 0.9 fusion.5
  156.9 15.3 %psum.29 = f32[48,48]{1,0:T(8,128)S(1)} all-reduce(f32[48,48]{1,0:T(8,128)S(1)} %fusion.5), channel_id=1, replica_groups=mesh['row'=4,'col'=8] {'row'}, use_global_device_ids=true, to_apply=%region_2.0 | all-reduce | flops 2304 | bytes 18432 | tf_op jit(solution)/shard_map/psum | solution.py:12
  173.6 1.5 cholesky.44
  176.4 1.2 custom-call.6
  178.6 39.3 %convolution_bitcast_fusion.4 = f32[4,576,16]{1,2,0:T(8,128)} fusion(f32[4,576,4608]{2,1,0:T(8,128)} %param.6, f32[16,4608]{1,0:T(8,128)S(1)} %fusion.23), kind=kOutput, calls=%fused_computation.10 | convolution fusion | flops 2038431744 | bytes 42909696 | tf_op jit(solution)/shard_map/aig,gk->aik/dot_general | solution.py:32
  218.1 8.7 %all-gather.4 = f32[4,576,16]{1,2,0:T(8,128)S(1)} all-gather(f32[1,576,16]{1,2,0:T(8,128)S(1)} %dynamic-slice_bitcast_fusion.1), channel_id=1, replica_groups=mesh['row'=4,'col'=8] {'row'}, dimensions={0}, use_global_device_ids=true | all-gather | bytes 184320 | tf_op jit(solution)/shard_map/all_gather | solution.py:29
  226.8 24.6 %convolution_bitcast_fusion.2 = f32[4608,16]{0,1:T(8,128)} fusion(f32[4,576,16]{1,2,0:T(8,128)S(1)} %all-gather.4, f32[4,576,4608]{2,1,0:T(8,128)} %param.6), kind=kOutput, calls=%fused_computation.8 | convolution fusion | flops 2038431744 | bytes 42909696 | tf_op jit(solution)/shard_map/aig,aik->gk/dot_general | solution.py:37
  252.4 28.0 %all-gather.1 = f32[1,4608,16]{2,0,1:T(1,128)S(1)} all-gather(f32[1,576,16]{2,0,1:T(1,128)S(1)} %copy.15), channel_id=3, replica_groups=mesh['row'=4,'col'=8] {'col'}, dimensions={1}, use_global_device_ids=true | all-gather | bytes 331776 | tf_op jit(solution)/shard_map/all_gather | solution.py:39
  280.4 2.2 copy.16
  282.6 24.1 %all-reduce.8.cloned.1.call-done = f32[4608,16]{0,1:T(8,128)} async-done(((f32[4608,16]{0,1:T(8,128)}), f32[4608,16]{0,1:T(8,128)}) %all-reduce.8.cloned.1.call-update) | async-done | bytes 294928 | tf_op jit(solution)/shard_map/psum | solution.py:38
  306.7 1.1 fusion.17
  308.6 16.3 %psum.31 = f32[48,48]{1,0:T(8,128)S(1)} all-reduce(f32[48,48]{1,0:T(8,128)S(1)} %fusion.10), channel_id=1, replica_groups=mesh['row'=4,'col'=8] {'row'}, use_global_device_ids=true, to_apply=%region_8.11 | all-reduce | flops 2304 | bytes 18432 | tf_op jit(solution)/shard_map/psum | solution.py:12
  326.1 1.5 cholesky.55
  328.9 1.2 custom-call.7
  331.8 1.3 pad_maximum_fusion
  (58 shorter events, 11.4 us)
Async XLA Ops:
  8.0 119.2 %reduce-scatter.7.cloned.1.call-start = ((), (), s32[]{:S(2)}) async-start(), calls=%async_computation.4 | async-start | bytes 204800
  24.5 73.8 %copy-start.2 = (u32[32]{0:T(128)S(1)}, u32[32]{0:T(128)}, u32[]{:S(2)}) copy-start(u32[32]{0:T(128)} %constant.50) | copy-start | bytes 388
  24.5 75.1 %copy-start.1 = (f32[576]{0:T(1024)S(1)}, f32[576]{0:T(1024)}, u32[]{:S(2)}) copy-start(f32[576]{0:T(1024)} %param.7) | copy-start | bytes 6916
  64.6 90.3 %all-reduce.6.cloned.1.call-start = ((), (), s32[]{:S(2)}) async-start(), calls=%async_computation.2 | async-start | bytes 589824 | tf_op jit(solution)/shard_map/psum | solution.py:38
  98.3 153.2 %reduce-scatter.9.cloned.1.call-start = ((), (), s32[]{:S(2)}) async-start(), calls=%async_computation.5 | async-start | bytes 204800
  127.2 124.2 %copy-start = (f32[4608]{0:T(1024)}, f32[4608]{0:T(1024)S(1)}, u32[]{:S(2)}) copy-start(f32[4608]{0:T(1024)S(1)} %all-reduce) | copy-start | bytes 55300
  218.0 88.7 %all-reduce.8.cloned.1.call-start = ((), (), s32[]{:S(2)}) async-start(), calls=%async_computation.3 | async-start | bytes 589824 | tf_op jit(solution)/shard_map/psum | solution.py:38
Sparse Core Ops, SparseCore 0:
  64.7 25.2 reduce-scatter.6
  218.1 24.4 reduce-scatter.8
Sparse Core Ops, SparseCore 1:
  98.3 55.3 all-reduce.5
  251.5 55.1 all-reduce.7
where the time goes:
time: 341 us
  blocking collectives  145 us (43%)
  matrix products  134 us (39%)
  waiting for transfers between devices  24.2 us (7%)
  between operations  16.4 us (5%)
  other arithmetic  12.2 us (4%)
  local copies, waits for them, and re-layouts  8.71 us (3%)
    dot_general x2, matrix products, on_device(): jnp.einsum('aig,gk->aik', coupling, column_block, precision=precise)  79.3 us
    all_gather x2, blocking collectives, on_device(): direct_rows = lax.all_gather(direct, 'col', axis=0, tiled=True)  52.6 us
    dot_general x2, matrix products, on_device(): jnp.einsum('aig,aik->gk', coupling, spread, precision=precise)  49.2 us
    psum x2, blocking collectives, combined(): return lax.psum(moments_local, 'row')  31.6 us
    unnamed x1, blocking collectives  27.3 us
    psum x2, waiting for transfers between devices, on_device(): transposed = lax.psum(partial_value, 'col')  24.1 us
    all_gather x2, blocking collectives, on_device(): spread = lax.all_gather(own_rows, 'row', axis=0, tiled=True)  17.5 us
    all_gather x1, blocking collectives, on_device(): lax.all_gather(block, 'col', axis=0, tiled=True)  16.3 us
  transfers between devices with their start and end apart: 4, of which 1 were waited for; matrix products, arithmetic and copies ran while one was open for 17% of the time, Pallas kernels for 0%

commit v1 on v0

--- a/solution.py
+++ b/solution.py
@@ -36,7 +36,25 @@
         ).reshape(segment, width)
         partial_value = jnp.einsum("aig,aik->gk", coupling, spread, precision=precise)
         transposed = lax.psum(partial_value, "col")
-        direct_rows = lax.all_gather(direct, "col", axis=0, tiled=True)
+        ways, here, hop = (lax.axis_size("col"), lax.axis_index("col"), direct.shape[0])
+        lengths = [n * ways if d == 0 else n for d, n in enumerate(direct.shape)]
+        full = lax.dynamic_update_slice_in_dim(
+            jnp.zeros(lengths, direct.dtype), direct, here * hop, axis=0
+        )
+        going_up = going_down = direct
+        for far in range(1, ways // 2 + 1):
+            going_up = lax.ppermute(going_up, "col", [(d, (d + 1) % ways) for d in range(ways)])
+            full = lax.dynamic_update_slice_in_dim(
+                full, going_up, (here - far) % ways * hop, axis=0
+            )
+            if 2 * far < ways:
+                going_down = lax.ppermute(
+                    going_down, "col", [(d, (d - 1) % ways) for d in range(ways)]
+                )
+                full = lax.dynamic_update_slice_in_dim(
+                    full, going_down, (here + far) % ways * hop, axis=0
+                )
+        direct_rows = full
         product = energy_rows[:, None] * current + direct_rows + transposed
         stacked = jnp.concatenate([current, prior, product], axis=1)
         moments = combined(jnp.einsum("nk,nl->kl", stacked, stacked, precision=precise)) / N

time: 341 us -> 391 us (1.15); the launches traced: 341 us -> 384 us
  waiting for transfers between devices: 24.2 us -> 96.1 us
  blocking collectives: 145 us -> 94.4 us
  starting transfers between devices: 0.17 us -> 20.3 us
    all_gather x2 -> x0, blocking collectives: 52.6 us -> none  [on_device(): direct_rows = lax.all_gather(direct, 'col', axis=0, tiled=True)]
    unnamed x6, waiting for transfers between devices: 0.09 us -> 41.7 us
    psum x2, waiting for transfers between devices: 24.1 us -> 47.8 us  [on_device(): transposed = lax.psum(partial_value, 'col')]
    ppermute x0 -> x14, starting transfers between devices: none -> 20.2 us  [the longest x6 19.5 us: on_device(): lax.ppermute(going_down, 'col', [(d, (d - 1) % ways) for d in range(ways)])]
    dynamic_update_slice x0 -> x16, local copies, waits for them, and re-layouts: none -> 9.22 us  [the longest x8 4.4 us: on_device(): lax.dynamic_update_slice_in_dim(full, going_up, (here - far) % ways * hop...]
    ppermute x0 -> x14, waiting for transfers between devices: none -> 6.69 us  [the longest x8 3.45 us: on_device(): lax.ppermute(going_up, 'col', [(d, (d + 1) % ways) for d in range(ways)])]
    all_gather x2 -> x0, local copies, waits for them, and re-layouts: 4.31 us -> none  [on_device(): direct_rows = lax.all_gather(direct, 'col', axis=0, tiled=True)]
  transfers between devices with their start and end apart: 4 -> 18, of which waited for: 1 -> 10; matrix products, arithmetic and copies ran while one was open for 17% -> 15% of each run, Pallas kernels for 0% -> 0%
where the time goes in v1:
time: 391 us; the launch traced here: 384 us
  matrix products  133 us (34%)
  waiting for transfers between devices  96.1 us (25%)
  blocking collectives  94.4 us (24%)
  starting transfers between devices  20.3 us (5%)
  between operations  16.9 us (4%)
  local copies, waits for them, and re-layouts  11.8 us (3%)
  other arithmetic  10.9 us (3%)
    dot_general x2, matrix products, on_device(): jnp.einsum('aig,gk->aik', coupling, column_block, precision=precise)  79.3 us
    dot_general x2, matrix products, on_device(): jnp.einsum('aig,aik->gk', coupling, spread, precision=precise)  49 us
    psum x2, waiting for transfers between devices, on_device(): transposed = lax.psum(partial_value, 'col')  47.8 us
    unnamed x6, waiting for transfers between devices  41.7 us
    psum x2, blocking collectives, combined(): return lax.psum(moments_local, 'row')  32.8 us
    unnamed x1, blocking collectives  29.1 us
    ppermute x6, starting transfers between devices, on_device(): lax.ppermute(going_down, 'col', [(d, (d - 1) % ways) for d in range(ways)])  19.5 us
    all_gather x1, blocking collectives, on_device(): lax.all_gather(block, 'col', axis=0, tiled=True)  16.3 us
  transfers between devices with their start and end apart: 18, of which 10 were waited for; matrix products, arithmetic and copies ran while one was open for 15% of the time, Pallas kernels for 0%

profile of v1, /device:TPU:0, one launch (start us, length us, event | category | flops | bytes accessed | tf_op | source)
XLA Modules:
  0.0 383.8 jit_solution(12315248957836721143)
XLA Ops:
  8.0 16.3 %all-gather = f32[8,576,16]{1,2,0:T(8,128)S(1)} all-gather(f32[1,576,16]{1,2,0:T(8,128)} %bitcast.93), channel_id=1, replica_groups=mesh['row'=4,'col'=8] {'col'}, dimensions={0}, use_global_device_ids=true | all-gather | bytes 331776 | tf_op jit(solution)/shard_map/all_gather | solution.py:20
  24.6 40.0 %fusion.42 = f32[4,576,16]{1,2,0:T(8,128)} fusion(f32[4,576,4608]{2,1,0:T(8,128)} %param.6, f32[4608,16,1]{0,1,2:T(8,128)S(1)} %reshape.44), kind=kOutput, calls=%fused_computation.75 | convolution fusion | flops 2038431744 | bytes 42909696 | tf_op jit(solution)/shard_map/aig,gk->aik/dot_general | solution.py:32
  64.7 25.4 %reduce-scatter.7.cloned.1.call-done = f32[1,576,16]{1,2,0:T(8,128)} async-done(((f32[4,576,16]{1,2,0:T(8,128)}), f32[1,576,16]{1,2,0:T(8,128)}) %reduce-scatter.7.cloned.1.call-update) | async-done | bytes 36880
  90.2 3.6 collective-permute-start.1
  93.8 1.7 collective-permute-done
  95.6 8.5 %all-gather.1 = f32[4,576,16]{1,2,0:T(8,128)S(1)} all-gather(f32[1,576,16]{1,2,0:T(8,128)S(1)} %dynamic-slice_bitcast_fusion.2), channel_id=1, replica_groups=mesh['row'=4,'col'=8] {'row'}, dimensions={0}, use_global_device_ids=true | all-gather | bytes 184320 | tf_op jit(solution)/shard_map/all_gather | solution.py:29
  104.1 1.6 collective-permute-start.3
  106.2 24.5 %convolution_bitcast_fusion.3 = f32[4608,16]{0,1:T(8,128)} fusion(f32[4,576,16]{1,2,0:T(8,128)S(1)} %all-gather.1, f32[4,576,4608]{2,1,0:T(8,128)} %param.6), kind=kOutput, calls=%fused_computation.9 | convolution fusion | flops 2038431744 | bytes 42909696 | tf_op jit(solution)/shard_map/aig,aik->gk/dot_general | solution.py:37
  130.8 3.6 collective-permute-start.5
  136.1 29.1 %all-reduce = f32[4608]{0:T(1024)S(1)} all-reduce(f32[4608]{0:T(1024)S(1)} %dynamic-update-slice.2), channel_id=1, replica_groups=mesh['row'=4,'col'=8] {'col'}, use_global_device_ids=true, to_apply=%add | all-reduce | flops 4608 | bytes 36864
  170.0 14.1 %all-reduce.6.cloned.1.call-done = f32[4608,16]{0,1:T(8,128)} async-done(((f32[4608,16]{0,1:T(8,128)}), f32[4608,16]{0,1:T(8,128)}) %all-reduce.6.cloned.1.call-update) | async-done | bytes 294928 | tf_op jit(solution)/shard_map/psum | solution.py:38
  186.0 16.6 %psum.29 = f32[48,48]{1,0:T(8,128)S(1)} all-reduce(f32[48,48]{1,0:T(8,128)S(1)} %fusion.5), channel_id=1, replica_groups=mesh['row'=4,'col'=8] {'row'}, use_global_device_ids=true, to_apply=%region_2.3 | all-reduce | flops 2304 | bytes 18432 | tf_op jit(solution)/shard_map/psum | solution.py:12
  203.3 1.5 cholesky.44
  208.4 39.3 %convolution_bitcast_fusion.4 = f32[4,576,16]{1,2,0:T(8,128)} fusion(f32[4,576,4608]{2,1,0:T(8,128)} %param.6, f32[16,4608]{1,0:T(8,128)S(1)} %fusion.21), kind=kOutput, calls=%fused_computation.10 | convolution fusion | flops 2038431744 | bytes 42909696 | tf_op jit(solution)/shard_map/aig,gk->aik/dot_general | solution.py:32
  247.8 7.7 %all-gather.2 = f32[4,576,16]{1,2,0:T(8,128)S(1)} all-gather(f32[1,576,16]{1,2,0:T(8,128)S(1)} %dynamic-slice_bitcast_fusion.1), channel_id=1, replica_groups=mesh['row'=4,'col'=8] {'row'}, dimensions={0}, use_global_device_ids=true | all-gather | bytes 184320 | tf_op jit(solution)/shard_map/all_gather | solution.py:29
  255.5 16.2 %reduce-scatter.9.cloned.1.call-done = f32[1,576,16]{1,2,0:T(8,128)} async-done(((f32[4,576,16]{1,2,0:T(8,128)}), f32[1,576,16]{1,2,0:T(8,128)}) %reduce-scatter.9.cloned.1.call-update) | async-done | bytes 36880
  271.9 24.5 %convolution_bitcast_fusion.2 = f32[4608,16]{0,1:T(8,128)} fusion(f32[4,576,16]{1,2,0:T(8,128)S(1)} %all-gather.2, f32[4,576,4608]{2,1,0:T(8,128)} %param.6), kind=kOutput, calls=%fused_computation.8 | convolution fusion | flops 2038431744 | bytes 42909696 | tf_op jit(solution)/shard_map/aig,aik->gk/dot_general | solution.py:37
  296.5 3.6 collective-permute-start.8
  300.0 1.7 collective-permute-done.8
  301.7 3.5 collective-permute-start.10
  305.4 1.6 collective-permute-done.10
  306.9 3.7 collective-permute-start.12
  316.8 33.6 %all-reduce.8.cloned.1.call-done = f32[4608,16]{0,1:T(8,128)} async-done(((f32[4608,16]{0,1:T(8,128)}), f32[4608,16]{0,1:T(8,128)}) %all-reduce.8.cloned.1.call-update) | async-done | bytes 294928 | tf_op jit(solution)/shard_map/psum | solution.py:38
  352.3 16.3 %psum.31 = f32[48,48]{1,0:T(8,128)S(1)} all-reduce(f32[48,48]{1,0:T(8,128)S(1)} %fusion.11), channel_id=1, replica_groups=mesh['row'=4,'col'=8] {'row'}, use_global_device_ids=true, to_apply=%region_8.11 | all-reduce | flops 2304 | bytes 18432 | tf_op jit(solution)/shard_map/psum | solution.py:12
  (98 shorter events, 28.8 us)
Async XLA Ops:
  8.0 82.1 %reduce-scatter.7.cloned.1.call-start = ((), (), s32[]{:S(2)}) async-start(), calls=%async_computation.4 | async-start | bytes 204800
  24.5 110.0 %copy-start.3 = (u32[32]{0:T(128)S(1)}, u32[32]{0:T(128)}, u32[]{:S(2)}) copy-start(u32[32]{0:T(128)} %constant.115) | copy-start | bytes 388
  24.5 111.2 %copy-start.2 = (f32[576]{0:T(1024)S(1)}, f32[576]{0:T(1024)}, u32[]{:S(2)}) copy-start(f32[576]{0:T(1024)} %param.7) | copy-start | bytes 6916
  64.6 119.5 %all-reduce.6.cloned.1.call-start = ((), (), s32[]{:S(2)}) async-start(), calls=%async_computation.2 | async-start | bytes 589824 | tf_op jit(solution)/shard_map/psum | solution.py:38
  90.1 75.2 %copy-start = (f32[1,576,16]{1,2,0:T(8,128)S(1)}, f32[1,576,16]{1,2,0:T(8,128)}, u32[]{:S(2)}) copy-start(f32[1,576,16]{1,2,0:T(8,128)} %reduce-scatter.7.cloned.1.call-done) | copy-start | bytes 110596
  90.1 5.5 %collective-permute-start = (f32[576,16]{0,1:T(8,128)}, f32[576,16]{0,1:T(8,128)S(1)}, u32[]{:S(2)}, u32[]{:S(2)}) collective-permute-start(f32[576,16]{0,1:T(8,128)} %bitcast.87), channel_id=1, source_target_pairs={{0,1},{1,2},{2,3},{3,4},{4,5},{5,6},{6,7},{7,0},{8,9},{9,10},{10,1... | collective-permute-start | bytes 110600 | tf_op jit(solution)/shard_map/ppermute | solution.py:46
  90.2 14.0 %collective-permute-start.1 = (f32[576,16]{0,1:T(8,128)}, f32[576,16]{0,1:T(8,128)S(1)}, u32[]{:S(2)}, u32[]{:S(2)}) collective-permute-start(f32[576,16]{0,1:T(8,128)} %bitcast.88), channel_id=1, source_target_pairs={{0,7},{1,0},{2,1},{3,2},{4,3},{5,4},{6,5},{7,6},{8,15},{9,8},{10,9... | collective-permute-start | bytes 110600 | tf_op jit(solution)/shard_map/ppermute | solution.py:51
  95.5 10.2 %collective-permute-start.2 = (f32[576,16]{0,1:T(8,128)S(1)}, f32[576,16]{0,1:T(8,128)S(1)}, u32[]{:S(2)}, u32[]{:S(2)}) collective-permute-start(f32[576,16]{0,1:T(8,128)S(1)} %collective-permute-done), channel_id=1, source_target_pairs={{0,1},{1,2},{2,3},{3,4},{4,5},{5,6},{6,7},{7,0},{8,9},{9,10},{10,1... | collective-permute-start | bytes 110600 | tf_op jit(solution)/shard_map/ppermute | solution.py:46
  104.1 26.6 %collective-permute-start.3 = (f32[576,16]{0,1:T(8,128)S(1)}, f32[576,16]{0,1:T(8,128)S(1)}, u32[]{:S(2)}, u32[]{:S(2)}) collective-permute-start(f32[576,16]{0,1:T(8,128)S(1)} %collective-permute-done.1), channel_id=1, source_target_pairs={{0,7},{1,0},{2,1},{3,2},{4,3},{5,4},{6,5},{7,6},{8,15},{9,8},{10,9... | collective-permute-start | bytes 110600 | tf_op jit(solution)/shard_map/ppermute | solution.py:51
  105.7 28.6 %collective-permute-start.4 = (f32[576,16]{0,1:T(8,128)S(1)}, f32[576,16]{0,1:T(8,128)S(1)}, u32[]{:S(2)}, u32[]{:S(2)}) collective-permute-start(f32[576,16]{0,1:T(8,128)S(1)} %collective-permute-done.2), channel_id=1, source_target_pairs={{0,1},{1,2},{2,3},{3,4},{4,5},{5,6},{6,7},{7,0},{8,9},{9,10},{10,1... | collective-permute-start | bytes 110600 | tf_op jit(solution)/shard_map/ppermute | solution.py:46
  130.7 141.0 %reduce-scatter.9.cloned.1.call-start = ((), (), s32[]{:S(2)}) async-start(), calls=%async_computation.5 | async-start | bytes 204800
  130.8 38.0 %collective-permute-start.5 = (f32[576,16]{0,1:T(8,128)S(1)}, f32[576,16]{0,1:T(8,128)S(1)}, u32[]{:S(2)}, u32[]{:S(2)}) collective-permute-start(f32[576,16]{0,1:T(8,128)S(1)} %collective-permute-done.3), channel_id=1, source_target_pairs={{0,7},{1,0},{2,1},{3,2},{4,3},{5,4},{6,5},{7,6},{8,15},{9,8},{10,9... | collective-permute-start | bytes 110600 | tf_op jit(solution)/shard_map/ppermute | solution.py:51
  134.4 35.1 %collective-permute-start.6 = (f32[576,16]{0,1:T(8,128)S(1)}, f32[576,16]{0,1:T(8,128)S(1)}, u32[]{:S(2)}, u32[]{:S(2)}) collective-permute-start(f32[576,16]{0,1:T(8,128)S(1)} %collective-permute-done.4), channel_id=1, source_target_pairs={{0,1},{1,2},{2,3},{3,4},{4,5},{5,6},{6,7},{7,0},{8,9},{9,10},{10,1... | collective-permute-start | bytes 110600 | tf_op jit(solution)/shard_map/ppermute | solution.py:46
  247.6 102.8 %all-reduce.8.cloned.1.call-start = ((), (), s32[]{:S(2)}) async-start(), calls=%async_computation.3 | async-start | bytes 589824 | tf_op jit(solution)/shard_map/psum | solution.py:38
  271.7 24.8 %copy-start.1 = (f32[1,576,16]{1,2,0:T(8,128)S(1)}, f32[1,576,16]{1,2,0:T(8,128)}, u32[]{:S(2)}) copy-start(f32[1,576,16]{1,2,0:T(8,128)} %reduce-scatter.9.cloned.1.call-done) | copy-start | bytes 110596
  271.7 28.3 %collective-permute-start.7 = (f32[576,16]{0,1:T(8,128)}, f32[576,16]{0,1:T(8,128)S(1)}, u32[]{:S(2)}, u32[]{:S(2)}) collective-permute-start(f32[576,16]{0,1:T(8,128)} %bitcast.90), channel_id=1, source_target_pairs={{0,1},{1,2},{2,3},{3,4},{4,5},{5,6},{6,7},{7,0},{8,9},{9,10},{10,1... | collective-permute-start | bytes 110600 | tf_op jit(solution)/shard_map/ppermute | solution.py:46
  296.5 5.2 %collective-permute-start.8 = (f32[576,16]{0,1:T(8,128)S(1)}, f32[576,16]{0,1:T(8,128)S(1)}, u32[]{:S(2)}, u32[]{:S(2)}) collective-permute-start(f32[576,16]{0,1:T(8,128)S(1)} %bitcast.91), channel_id=1, source_target_pairs={{0,7},{1,0},{2,1},{3,2},{4,3},{5,4},{6,5},{7,6},{8,15},{9,8},{10,9... | collective-permute-start | bytes 110600 | tf_op jit(solution)/shard_map/ppermute | solution.py:51
  300.0 5.3 %collective-permute-start.9 = (f32[576,16]{0,1:T(8,128)S(1)}, f32[576,16]{0,1:T(8,128)S(1)}, u32[]{:S(2)}, u32[]{:S(2)}) collective-permute-start(f32[576,16]{0,1:T(8,128)S(1)} %collective-permute-done.7), channel_id=1, source_target_pairs={{0,1},{1,2},{2,3},{3,4},{4,5},{5,6},{6,7},{7,0},{8,9},{9,10},{10,1... | collective-permute-start | bytes 110600 | tf_op jit(solution)/shard_map/ppermute | solution.py:46
  301.7 5.2 %collective-permute-start.10 = (f32[576,16]{0,1:T(8,128)S(1)}, f32[576,16]{0,1:T(8,128)S(1)}, u32[]{:S(2)}, u32[]{:S(2)}) collective-permute-start(f32[576,16]{0,1:T(8,128)S(1)} %collective-permute-done.8), channel_id=1, source_target_pairs={{0,7},{1,0},{2,1},{3,2},{4,3},{5,4},{6,5},{7,6},{8,15},{9,8},{10,9... | collective-permute-start | bytes 110600 | tf_op jit(solution)/shard_map/ppermute | solution.py:51
  305.4 5.6 %collective-permute-start.11 = (f32[576,16]{0,1:T(8,128)S(1)}, f32[576,16]{0,1:T(8,128)S(1)}, u32[]{:S(2)}, u32[]{:S(2)}) collective-permute-start(f32[576,16]{0,1:T(8,128)S(1)} %collective-permute-done.9), channel_id=1, source_target_pairs={{0,1},{1,2},{2,3},{3,4},{4,5},{5,6},{6,7},{7,0},{8,9},{9,10},{10,1... | collective-permute-start | bytes 110600 | tf_op jit(solution)/shard_map/ppermute | solution.py:46
  306.9 7.5 %collective-permute-start.12 = (f32[576,16]{0,1:T(8,128)S(1)}, f32[576,16]{0,1:T(8,128)S(1)}, u32[]{:S(2)}, u32[]{:S(2)}) collective-permute-start(f32[576,16]{0,1:T(8,128)S(1)} %collective-permute-done.10), channel_id=1, source_target_pairs={{0,7},{1,0},{2,1},{3,2},{4,3},{5,4},{6,5},{7,6},{8,15},{9,8},{10,9... | collective-permute-start | bytes 110600 | tf_op jit(solution)/shard_map/ppermute | solution.py:51
  311.0 5.3 %collective-permute-start.13 = (f32[576,16]{0,1:T(8,128)S(1)}, f32[576,16]{0,1:T(8,128)S(1)}, u32[]{:S(2)}, u32[]{:S(2)}) collective-permute-start(f32[576,16]{0,1:T(8,128)S(1)} %collective-permute-done.11), channel_id=1, source_target_pairs={{0,1},{1,2},{2,3},{3,4},{4,5},{5,6},{6,7},{7,0},{8,9},{9,10},{10,1... | collective-permute-start | bytes 110600 | tf_op jit(solution)/shard_map/ppermute | solution.py:46
Sparse Core Ops, SparseCore 0:
  64.7 25.2 reduce-scatter.6
  247.8 23.8 reduce-scatter.8
Sparse Core Ops, SparseCore 1:
  130.8 53.3 all-reduce.5
  296.5 53.9 all-reduce.7
